TPU v7x, 32 devices: a whole 2x2x4 slice. The times are simulated.
32 devices in a mesh: dp: 8 (over z, y), mp: 4 (over x, core).
Axes of the slice: x: 2, y: 2, z: 4, core: 2. Of those that a mesh axis runs over, the one named last changes fastest.
Arguments:
- tokens: bfloat16 [14592, 768], P(('dp', 'mp')), may hold values from -6 to 6
- caption_mask: int32 [64, 128], P('dp'), may hold values from 0 to 1, as said below
- region_counts: int32 [16], replicated, may hold values from 36 to 100, as said below
- group_ids: int32 [64], P('dp'), may hold values from 0 to 15, as said below
- query_weight: bfloat16 [768, 768], P(None, 'mp'), may hold values from -0.21875 to 0.21875
- query_bias: float32 [768], P('mp'), may hold values from -3 to 3
- key_weight: bfloat16 [768, 768], P(None, 'mp'), may hold values from -0.21875 to 0.21875
- value_weight: bfloat16 [768, 768], P(None, 'mp'), may hold values from -0.21875 to 0.21875
- value_bias: float32 [768], P('mp'), may hold values from -3 to 3
- out_weight: bfloat16 [768, 768], P('mp'), may hold values from -1.25 to 1.25
- out_bias: float32 [768], replicated, may hold values from -3 to 3
- attn_gain: float32 [768], replicated, may hold values from 0.5 to 1.5
- attn_shift: float32 [768], replicated, may hold values from -3 to 3
- up_weight: bfloat16 [768, 3072], P(None, 'mp'), may hold values from -0.21875 to 0.21875
- up_bias: float32 [3072], P('mp'), may hold values from -3 to 3
- down_weight: bfloat16 [3072, 768], P('mp'), may hold values from -0.109375 to 0.109375
- down_bias: float32 [768], replicated, may hold values from -3 to 3
- final_gain: float32 [768], replicated, may hold values from 0.5 to 1.5
- final_shift: float32 [768], replicated, may hold values from -3 to 3
- cotangent: bfloat16 [14592, 768], P(('dp', 'mp')), may hold values from -6 to 6
Outputs:
- layer_out: bfloat16 [14592, 768], P(('dp', 'mp'))
- grad_tokens: float32 [14592, 768], P(('dp', 'mp'))
- grad_query_weight: float32 [768, 768], P(None, 'mp')
- grad_query_bias: float32 [768], P('mp')
- grad_key_weight: float32 [768, 768], P(None, 'mp')
- grad_value_weight: float32 [768, 768], P(None, 'mp')
- grad_value_bias: float32 [768], P('mp')
- grad_out_weight: float32 [768, 768], P('mp')
- grad_out_bias: float32 [768], replicated
- grad_attn_gain: float32 [768], replicated
- grad_attn_shift: float32 [768], replicated
- grad_up_weight: float32 [768, 3072], P(None, 'mp')
- grad_up_bias: float32 [3072], P('mp')
- grad_down_weight: float32 [3072, 768], P('mp')
- grad_down_bias: float32 [768], replicated
- grad_final_gain: float32 [768], replicated
- grad_final_shift: float32 [768], replicated
Inputs may be any that keep to these rules, and one draw needn't show every extreme that they name: `caption_mask`: each row is ones followed by zeros, with at least one one; some row is all ones. `region_counts`: some image has exactly 100 regions. `group_ids`: each image is named by exactly 4 sequences.
All inputs are finite; a program needn't handle non-finite values.
Results may differ from a plain program's by a relative error of at most 0.015.
Values may be sent and summed in bfloat16 or wider, within the bound.
A program may use at most 128 MiB of HBM per device.

v0:
```python
import jax
import jax.numpy as jnp
from jax import lax
from jax.sharding import PartitionSpec as P

HEAD = 64
MAXREG = 100


EPS = 1e-12
ROOT_HALF = 0.7071067811865476
DENSITY = 0.3989422804014327
MASKED = -1e30


def key_valid(caption_mask, region_counts, group_ids):
    images = region_counts.shape[0]
    match = group_ids[:, None] == jnp.arange(images, dtype=jnp.int32)[None, :]
    regions = jnp.sum(jnp.where(match, region_counts[None, :], 0), axis=1)
    slots = jnp.arange(MAXREG, dtype=jnp.int32)
    return jnp.concatenate([caption_mask > 0, slots[None, :] < regions[:, None]], axis=1)


def norm_forward(total, gain, shift):
    mean = jnp.mean(total, axis=-1, keepdims=True)
    centered = total - mean
    inverse = lax.rsqrt(jnp.mean(centered * centered, axis=-1, keepdims=True) + EPS)
    scaled = centered * inverse
    return (scaled * gain + shift, scaled, inverse)


def norm_backward(grad, scaled, inverse, gain):
    weighted = grad * gain
    centered = weighted - jnp.mean(weighted, axis=-1, keepdims=True)
    return inverse * (centered - scaled * jnp.mean(weighted * scaled, axis=-1, keepdims=True))


def split_heads(block, seqs):
    return block.reshape(seqs, -1, block.shape[1] // HEAD, HEAD)


def masked_scores(query_heads, key_heads, valid):
    scores = jnp.einsum(
        "sqhd,skhd->shqk", query_heads, key_heads, preferred_element_type=jnp.float32
    ) * HEAD ** (-0.5)
    return jnp.where(valid[:, None, None, :], scores, MASKED)


def attend(query, keys, values, valid):
    seqs = valid.shape[0]
    value_heads = split_heads(values, seqs)
    scores = masked_scores(split_heads(query, seqs), split_heads(keys, seqs), valid)
    top = jnp.max(scores, axis=-1, keepdims=True)
    weights = jnp.exp(scores - top)
    total = jnp.sum(weights, axis=-1, keepdims=True)
    probs = (weights / total).astype(jnp.bfloat16)
    context = jnp.einsum("shqk,skhd->sqhd", probs, value_heads, preferred_element_type=jnp.float32)
    return (context.reshape(query.shape).astype(jnp.bfloat16), top + jnp.log(total))


def attend_backward(query, keys, values, valid, log_total, grad_context):
    seqs = valid.shape[0]
    query_heads = split_heads(query, seqs)
    key_heads = split_heads(keys, seqs)
    value_heads = split_heads(values, seqs)
    grad_heads = split_heads(grad_context, seqs)
    probs = jnp.exp(masked_scores(query_heads, key_heads, valid) - log_total)
    grad_values = jnp.einsum(
        "shqk,sqhd->skhd",
        probs.astype(jnp.bfloat16),
        grad_heads,
        preferred_element_type=jnp.float32,
    )
    grad_probs = jnp.einsum(
        "sqhd,skhd->shqk", grad_heads, value_heads, preferred_element_type=jnp.float32
    )
    row_total = jnp.sum(probs * grad_probs, axis=-1, keepdims=True)
    grad_scores = (probs * (grad_probs - row_total)).astype(jnp.bfloat16)
    scale = HEAD ** (-0.5)
    grad_query = (
        jnp.einsum("shqk,skhd->sqhd", grad_scores, key_heads, preferred_element_type=jnp.float32)
        * scale
    )
    grad_keys = (
        jnp.einsum("shqk,sqhd->skhd", grad_scores, query_heads, preferred_element_type=jnp.float32)
        * scale
    )
    shape = query.shape
    return (
        grad_query.reshape(shape).astype(jnp.bfloat16),
        grad_keys.reshape(shape).astype(jnp.bfloat16),
        grad_values.reshape(shape).astype(jnp.bfloat16),
    )


def attention_forward(
    tokens,
    valid,
    query_weight,
    query_bias,
    key_weight,
    value_weight,
    value_bias,
    out_weight,
    out_bias,
    attn_gain,
    attn_shift,
):
    whole = lax.all_gather(tokens, "mp", axis=0, tiled=True)
    query = (jnp.dot(whole, query_weight, preferred_element_type=jnp.float32) + query_bias).astype(
        jnp.bfloat16
    )
    keys = jnp.dot(whole, key_weight, preferred_element_type=jnp.float32).astype(jnp.bfloat16)
    values = (jnp.dot(whole, value_weight, preferred_element_type=jnp.float32) + value_bias).astype(
        jnp.bfloat16
    )
    context, log_total = attend(query, keys, values, valid)
    branch = lax.psum_scatter(
        jnp.dot(context, out_weight, preferred_element_type=jnp.float32),
        "mp",
        scatter_dimension=0,
        tiled=True,
    )
    normed, scaled, inverse = norm_forward(
        tokens.astype(jnp.float32) + branch + out_bias, attn_gain, attn_shift
    )
    return (whole, query, keys, values, context, log_total, normed, scaled, inverse)


def feedforward(normed, up_weight, up_bias, down_weight, down_bias, final_gain, final_shift):
    spread = lax.all_gather(normed.astype(jnp.bfloat16), "mp", axis=0, tiled=True)
    act_in = jnp.dot(spread, up_weight, preferred_element_type=jnp.float32) + up_bias
    cdf = 0.5 * (1.0 + jax.scipy.special.erf(act_in * ROOT_HALF))
    act = (act_in * cdf).astype(jnp.bfloat16)
    second = lax.psum_scatter(
        jnp.dot(act, down_weight, preferred_element_type=jnp.float32),
        "mp",
        scatter_dimension=0,
        tiled=True,
    )
    result, scaled, inverse = norm_forward(normed + second + down_bias, final_gain, final_shift)
    return (spread, act_in, act, result, scaled, inverse)


def body(
    tokens,
    caption_mask,
    region_counts,
    group_ids,
    query_weight,
    query_bias,
    key_weight,
    value_weight,
    value_bias,
    out_weight,
    out_bias,
    attn_gain,
    attn_shift,
    up_weight,
    up_bias,
    down_weight,
    down_bias,
    final_gain,
    final_shift,
    cotangent,
):
    valid = key_valid(caption_mask, region_counts, group_ids)
    first = attention_forward(
        tokens,
        valid,
        query_weight,
        query_bias,
        key_weight,
        value_weight,
        value_bias,
        out_weight,
        out_bias,
        attn_gain,
        attn_shift,
    )
    normed = first[6]
    second = feedforward(
        normed, up_weight, up_bias, down_weight, down_bias, final_gain, final_shift
    )
    layer_out = second[3].astype(jnp.bfloat16)
    second = feedforward(
        normed, up_weight, up_bias, down_weight, down_bias, final_gain, final_shift
    )
    spread, act_in, act, unused, scaled_out, inverse_out = second
    grad_out = cotangent.astype(jnp.float32)
    grad_final = norm_backward(grad_out, scaled_out, inverse_out, final_gain)
    final_gain_part = jnp.sum(grad_out * scaled_out, axis=0)
    final_shift_part = jnp.sum(grad_out, axis=0)
    grad_branch = lax.all_gather(grad_final.astype(jnp.bfloat16), "mp", axis=0, tiled=True)
    grad_down_weight = jnp.einsum("rf,rd->fd", act, grad_branch, preferred_element_type=jnp.float32)
    grad_down_bias = jnp.sum(grad_branch, axis=0, dtype=jnp.float32)
    grad_act = jnp.einsum("rd,fd->rf", grad_branch, down_weight, preferred_element_type=jnp.float32)
    cdf = 0.5 * (1.0 + jax.scipy.special.erf(act_in * ROOT_HALF))
    slope = cdf + act_in * jnp.exp(-0.5 * act_in * act_in) * DENSITY
    grad_in = (grad_act * slope).astype(jnp.bfloat16)
    grad_up_weight = jnp.einsum("rd,rf->df", spread, grad_in, preferred_element_type=jnp.float32)
    grad_up_bias = jnp.sum(grad_in, axis=0, dtype=jnp.float32)
    grad_mid = grad_final + lax.psum_scatter(
        jnp.einsum("rf,df->rd", grad_in, up_weight, preferred_element_type=jnp.float32),
        "mp",
        scatter_dimension=0,
        tiled=True,
    )
    upper_grads = (grad_up_weight, grad_up_bias, grad_down_weight, grad_down_bias)
    first = attention_forward(
        tokens,
        valid,
        query_weight,
        query_bias,
        key_weight,
        value_weight,
        value_bias,
        out_weight,
        out_bias,
        attn_gain,
        attn_shift,
    )
    whole, query, keys, values, context, log_total, unused_mid, scaled_mid, inverse_mid = first
    grad_first = norm_backward(grad_mid, scaled_mid, inverse_mid, attn_gain)
    attn_gain_part = jnp.sum(grad_mid * scaled_mid, axis=0)
    attn_shift_part = jnp.sum(grad_mid, axis=0)
    grad_attn = lax.all_gather(grad_first.astype(jnp.bfloat16), "mp", axis=0, tiled=True)
    grad_out_weight = jnp.einsum(
        "rc,rd->cd", context, grad_attn, preferred_element_type=jnp.float32
    )
    grad_out_bias = jnp.sum(grad_attn, axis=0, dtype=jnp.float32)
    grad_context = jnp.einsum(
        "rd,cd->rc", grad_attn, out_weight, preferred_element_type=jnp.float32
    ).astype(jnp.bfloat16)
    grad_query, grad_keys, grad_values = attend_backward(
        query, keys, values, valid, log_total, grad_context
    )
    grad_query_weight = jnp.einsum(
        "rd,rc->dc", whole, grad_query, preferred_element_type=jnp.float32
    )
    grad_query_bias = jnp.sum(grad_query, axis=0, dtype=jnp.float32)
    grad_key_weight = jnp.einsum("rd,rc->dc", whole, grad_keys, preferred_element_type=jnp.float32)
    grad_value_weight = jnp.einsum(
        "rd,rc->dc", whole, grad_values, preferred_element_type=jnp.float32
    )
    grad_value_bias = jnp.sum(grad_values, axis=0, dtype=jnp.float32)
    total = jnp.einsum("rc,dc->rd", grad_query, query_weight, preferred_element_type=jnp.float32)
    total = total + jnp.einsum(
        "rc,dc->rd", grad_keys, key_weight, preferred_element_type=jnp.float32
    )
    grad_tokens = grad_first + lax.psum_scatter(
        (
            total
            + jnp.einsum("rc,dc->rd", grad_values, value_weight, preferred_element_type=jnp.float32)
        ).astype(jnp.bfloat16),
        "mp",
        scatter_dimension=0,
        tiled=True,
    ).astype(jnp.float32)
    norm_sums = lax.psum(
        (attn_gain_part, attn_shift_part, final_gain_part, final_shift_part), ("dp", "mp")
    )
    summed = lax.psum(
        (
            grad_query_weight,
            grad_query_bias,
            grad_key_weight,
            grad_value_weight,
            grad_value_bias,
            grad_out_weight,
            grad_out_bias,
            grad_up_weight,
            grad_up_bias,
            grad_down_weight,
            grad_down_bias,
        ),
        "dp",
    )
    lower_grads = summed[:7]
    upper_grads = summed[7:]
    return (
        layer_out,
        grad_tokens,
        lower_grads[0],
        lower_grads[1],
        lower_grads[2],
        lower_grads[3],
        lower_grads[4],
        lower_grads[5],
        lower_grads[6],
        norm_sums[0],
        norm_sums[1],
        upper_grads[0],
        upper_grads[1],
        upper_grads[2],
        upper_grads[3],
        norm_sums[2],
        norm_sums[3],
    )


def solution(mesh):
    return jax.shard_map(
        body,
        mesh=mesh,
        in_specs=(
            P(("dp", "mp"), None),
            P("dp", None),
            P(),
            P("dp"),
            P(None, "mp"),
            P("mp"),
            P(None, "mp"),
            P(None, "mp"),
            P("mp"),
            P("mp", None),
            P(),
            P(),
            P(),
            P(None, "mp"),
            P("mp"),
            P("mp", None),
            P(),
            P(),
            P(),
            P(("dp", "mp"), None),
        ),
        out_specs=(
            P(("dp", "mp"), None),
            P(("dp", "mp"), None),
            P(None, "mp"),
            P("mp"),
            P(None, "mp"),
            P(None, "mp"),
            P("mp"),
            P("mp", None),
            P(),
            P(),
            P(),
            P(None, "mp"),
            P("mp"),
            P("mp", None),
            P(),
            P(),
            P(),
        ),
        check_vma=False,
    )
```

profile of v0, /device:TPU:0, one launch (start us, length us, event | category | flops | bytes accessed | tf_op | source)
XLA Modules:
  0.0 669.7 jit_solution(431593237311319448)
XLA Ops:
  9.6 29.3 %all-gather.5.cloned.1.call-done = bf16[1824,768]{1,0:T(8,128)(2,1)} async-done(((bf16[456,768]{1,0:T(8,128)(2,1)}), bf16[1824,768]{1,0:T(8,128)(2,1)}) %all-gather.5.cloned.1.call-update) | async-done | bytes 2801680 | tf_op jit(solution)/shard_map/all_gather | solution.py:109
  38.9 2.9 convolution_convert_fusion.1
  43.2 3.2 fusion.13
  47.7 4.1 fusion.12
  61.3 4.4 fusion.44
  65.8 53.7 %reduce-scatter.5.cloned.1.call-done = f32[456,768]{1,0:T(8,128)} async-done(((f32[1824,768]{1,0:T(8,128)}), f32[456,768]{1,0:T(8,128)}) %reduce-scatter.5.cloned.1.call-update) | async-done | bytes 1400848 | tf_op jit(solution)/shard_map/reduce_scatter | solution.py:118
  123.0 26.5 %all-gather.7.cloned.1.call-done = bf16[1824,768]{1,0:T(8,128)(2,1)} async-done(((bf16[456,768]{1,0:T(8,128)(2,1)}), bf16[1824,768]{1,0:T(8,128)(2,1)}) %all-gather.7.cloned.1.call-update) | async-done | bytes 2801680 | tf_op jit(solution)/shard_map/all_gather | solution.py:131
  149.5 6.4 multiply_convert_fusion.1
  157.5 4.8 fusion.45
  162.4 53.8 %reduce-scatter.7.cloned.1.call-done = f32[456,768]{1,0:T(8,128)} async-done(((f32[1824,768]{1,0:T(8,128)}), f32[456,768]{1,0:T(8,128)}) %reduce-scatter.7.cloned.1.call-update) | async-done | bytes 1400848 | tf_op jit(solution)/shard_map/reduce_scatter | solution.py:135
  220.5 26.7 %all-gather.9.cloned.1.call-done = bf16[1824,768]{1,0:T(8,128)(2,1)} async-done(((bf16[456,768]{1,0:T(8,128)(2,1)}), bf16[1824,768]{1,0:T(8,128)(2,1)}) %all-gather.9.cloned.1.call-update) | async-done | bytes 2801680 | tf_op jit(solution)/shard_map/all_gather | solution.py:194
  247.2 6.3 convert_reduce_fusion.1
  255.2 4.9 fusion.46
  260.1 53.8 %reduce-scatter.9.cloned.1.call-done = f32[456,768]{1,0:T(8,128)} async-done(((f32[1824,768]{1,0:T(8,128)}), f32[456,768]{1,0:T(8,128)}) %reduce-scatter.9.cloned.1.call-update) | async-done | bytes 1400848 | tf_op jit(solution)/shard_map/reduce_scatter | solution.py:203
  313.9 3.8 multiply_reduce_fusion.1
  319.8 26.4 %all-gather.11.cloned.1.call-done = bf16[1824,768]{1,0:T(8,128)(2,1)} async-done(((bf16[456,768]{1,0:T(8,128)(2,1)}), bf16[1824,768]{1,0:T(8,128)(2,1)}) %all-gather.11.cloned.1.call-update) | async-done | bytes 2801680 | tf_op jit(solution)/shard_map/all_gather | solution.py:227
  346.2 2.9 convolution_convert_fusion
  350.4 3.9 convert_reduce_fusion.4
  354.4 4.4 multiply_reduce_fusion
  377.9 6.9 %fusion.51 = f32[768,768]{1,0:T(8,128)} fusion(bf16[1824,768]{1,0:T(8,128)(2,1)} %copy-done.39, bf16[1824,768]{1,0:T(8,128)(2,1)} %all-gather.9.cloned.1.call-done), kind=kOutput, calls=%fused_computation.101 | convolution fusion | flops 2151677952 | bytes 7962624 | tf_op jit(solution)/shard_map/rf,rd->fd/dot_general | solution.py:195
  384.8 4.1 fusion.50
  398.3 41.6 %all-reduce = (f32[768]{0:T(1024)}, f32[768]{0:T(1024)}, f32[768]{0:T(1024)}, f32[768]{0:T(1024)}) all-reduce(f32[768]{0:T(1024)S(1)} %get-tuple-element.17, f32[768]{0:T(1024)S(1)} %get-tuple-element.22, f32[768]{0:T(1024)S(1)} %get-tuple-element.19, f32[768]{0:T(1024)S(1)} %get-tuple-element.24), channel_id=1, replica_groups=mesh['dp'=8,'mp'=4] {'dp','mp'}, use_global_device_ids=true, to_apply=%region_27.28 | all-reduce | flops 3072 | bytes 24576 | tf_op jit(solution)/shard_map/psum | solution.py:260
  442.4 39.6 %all-reduce.1 = (f32[192]{0:T(256)}, f32[192]{0:T(256)}, f32[768]{0:T(1024)}, f32[768]{0:T(1024)}, f32[768]{0:T(1024)}) all-reduce(f32[192]{0:T(256)S(1)} %reduce_sum.216, f32[192]{0:T(256)S(1)} %reduce_sum.218, f32[768]{0:T(1024)S(1)} %convert_reduce_fusion.2, ...), channel_id=1, replica_groups=mesh['dp'=8,'mp'=4] {'dp'}, use_global_device_ids=true, to_apply=%region_18.19 | all-reduce | flops 2688 | bytes 21504 | tf_op jit(solution)/shard_map/psum | solution.py:263
  484.3 168.9 %all-reduce.5.cloned.1.call-done = (f32[768,192]{0,1:T(8,128)}, f32[768,192]{0,1:T(8,128)}, f32[768,192]{0,1:T(8,128)}, f32[192,768]{1,0:T(8,128)}, f32[768,768]{1,0:T(8,128)}, /*index=5*/f32[768,768]{1,0:T(8,128)}) async-done(((f32[768,192]{0,1:T(8,128)}, f32[768,192]{0,1:T(8,128)}, f32[768,192]{0,1:T(8,128)}, f32[192,768]{1,0:T(8,128)}, f32[768,768]{1,0:T(8,128)}, /*index=5*/f32[768,768]{1,0:T(8,128)}), ...) | async-done | bytes 7077904 | tf_op jit(solution)/shard_map/psum | solution.py:263
  (164 shorter events, 71.6 us)
Async XLA Ops:
  7.2 142.3 %copy-start = (bf16[768,768]{1,0:T(8,128)(2,1)S(1)}, bf16[768,768]{1,0:T(8,128)(2,1)}, u32[]{:S(2)}) copy-start(bf16[768,768]{1,0:T(8,128)(2,1)} %param.33) | copy-start | bytes 3538948
  7.2 31.7 %all-gather.5.cloned.1.call-start = ((), (), s32[]{:S(2)}) async-start(), calls=%async_computation.4 | async-start | bytes 3502080 | tf_op jit(solution)/shard_map/all_gather | solution.py:109
  7.9 111.6 %reduce-scatter.5.cloned.1.call-start = ((), (), s32[]{:S(2)}) async-start(), calls=%async_computation.5 | async-start | bytes 7004160 | tf_op jit(solution)/shard_map/reduce_scatter | solution.py:118
  9.6 33.5 %copy-start.37 = (f32[192]{0:T(256)S(1)}, f32[192]{0:T(256)}, u32[]{:S(2)}) copy-start(f32[192]{0:T(256)} %param.25) | copy-start | bytes 2308
  43.1 11.2 %copy-start.6 = (bf16[8,228,3,64]{1,0,3,2:T(8,128)(2,1)}, bf16[8,228,3,64]{1,0,3,2:T(8,128)(2,1)S(1)}, u32[]{:S(2)}) copy-start(bf16[8,228,3,64]{1,0,3,2:T(8,128)(2,1)S(1)} %reshape.129) | copy-start | bytes 2101252
  65.7 53.8 %copy-start.31 = (f32[768]{0:T(1024)S(1)}, f32[768]{0:T(1024)}, u32[]{:S(2)}) copy-start(f32[768]{0:T(1024)} %param.30) | copy-start | bytes 9220
  65.7 55.9 %copy-start.28 = (f32[768]{0:T(1024)S(1)}, f32[768]{0:T(1024)}, u32[]{:S(2)}) copy-start(f32[768]{0:T(1024)} %param.31) | copy-start | bytes 9220
  65.7 55.9 %copy-start.30 = (f32[768]{0:T(1024)S(1)}, f32[768]{0:T(1024)}, u32[]{:S(2)}) copy-start(f32[768]{0:T(1024)} %param.32) | copy-start | bytes 9220
  65.7 83.8 %all-gather.7.cloned.1.call-start = ((), (), s32[]{:S(2)}) async-start(), calls=%async_computation.6 | async-start | bytes 3502080 | tf_op jit(solution)/shard_map/all_gather | solution.py:131
  121.3 28.2 %copy-start.36 = (f32[768]{0:T(1024)S(1)}, f32[768]{0:T(1024)}, u32[]{:S(2)}) copy-start(f32[768]{0:T(1024)} %param.34) | copy-start | bytes 9220
  122.8 93.3 %reduce-scatter.7.cloned.1.call-start = ((), (), s32[]{:S(2)}) async-start(), calls=%async_computation.7 | async-start | bytes 7004160 | tf_op jit(solution)/shard_map/reduce_scatter | solution.py:135
  149.5 7.9 %copy-start.35 = (bf16[768,768]{1,0:T(8,128)(2,1)S(1)}, bf16[768,768]{1,0:T(8,128)(2,1)}, u32[]{:S(2)}) copy-start(bf16[768,768]{1,0:T(8,128)(2,1)} %param.35) | copy-start | bytes 3538948
  162.3 53.8 %copy-start.33 = (f32[768]{0:T(1024)S(1)}, f32[768]{0:T(1024)}, u32[]{:S(2)}) copy-start(f32[768]{0:T(1024)} %param.36) | copy-start | bytes 9220
  162.3 56.1 %copy-start.29 = (f32[768]{0:T(1024)S(1)}, f32[768]{0:T(1024)}, u32[]{:S(2)}) copy-start(f32[768]{0:T(1024)} %param.37) | copy-start | bytes 9220
  162.3 84.9 %all-gather.9.cloned.1.call-start = ((), (), s32[]{:S(2)}) async-start(), calls=%async_computation.8 | async-start | bytes 3502080 | tf_op jit(solution)/shard_map/all_gather | solution.py:194
  220.5 93.4 %reduce-scatter.9.cloned.1.call-start = ((), (), s32[]{:S(2)}) async-start(), calls=%async_computation.9 | async-start | bytes 7004160 | tf_op jit(solution)/shard_map/reduce_scatter | solution.py:203
  260.0 53.8 %copy-start.13 = (bf16[456,768]{1,0:T(8,128)(2,1)S(1)}, bf16[456,768]{1,0:T(8,128)(2,1)}, u32[]{:S(2)}) copy-start(bf16[456,768]{1,0:T(8,128)(2,1)} %param.39) | copy-start | bytes 2101252
  260.0 53.8 %copy-start.32 = (f32[768]{0:T(1024)S(1)}, f32[768]{0:T(1024)}, u32[]{:S(2)}) copy-start(f32[768]{0:T(1024)} %param.38) | copy-start | bytes 9220
  260.1 86.1 %all-gather.11.cloned.1.call-start = ((), (), s32[]{:S(2)}) async-start(), calls=%async_computation.10 | async-start | bytes 3502080 | tf_op jit(solution)/shard_map/all_gather | solution.py:227
  317.7 28.5 %copy-start.22 = (bf16[192,768]{1,0:T(8,128)(2,1)S(1)}, bf16[192,768]{1,0:T(8,128)(2,1)}, u32[]{:S(2)}) copy-start(bf16[192,768]{1,0:T(8,128)(2,1)} %param.29) | copy-start | bytes 884740
  319.5 162.5 %reduce-scatter.11.cloned.1.call-start = ((), (), s32[]{:S(2)}) async-start(), calls=%async_computation.11 | async-start | bytes 3502080 | tf_op jit(solution)/shard_map/reduce_scatter | solution.py:251
  350.4 8.4 %slice-start = ((s8[5701632]{0:T(1024)(128)(4,1)}), s8[4194304]{0:T(1024)(128)(4,1)S(1)}, s32[]{:S(2)}) async-start(s8[5701632]{0:T(1024)(128)(4,1)} %bitcast.74), calls=%async_computation.13 | async-start | bytes 8388608
  377.9 275.3 %all-reduce.5.cloned.1.call-start = ((), (), s32[]{:S(2)}) async-start(), calls=%async_computation.12 | async-start | bytes 14155776 | tf_op jit(solution)/shard_map/psum | solution.py:263
  395.9 86.1 %copy-start.14 = (f32[456,768]{1,0:T(8,128)S(1)}, f32[456,768]{1,0:T(8,128)}, u32[]{:S(2)}) copy-start(f32[456,768]{1,0:T(8,128)} %get-tuple-element.41) | copy-start | bytes 4202500
  (29 other events, 92.5 us)
Sparse Core Ops, SparseCore 0:
  9.6 29.2 all-gather.4
  65.8 53.6 reduce-scatter.4
  122.9 26.5 all-gather.6
  162.4 53.6 reduce-scatter.6
  220.6 26.5 all-gather.8
  260.2 53.6 reduce-scatter.8
  319.6 26.5 all-gather.10
  378.0 36.2 reduce-scatter.10
  420.5 232.6 all-reduce.4
where the time goes:
time: 678 us; the launch traced here: 670 us
  waiting for transfers between devices  440 us (65%)
  blocking collectives  81.2 us (12%)
  matrix products  76.6 us (11%)
  local copies, waits for them, and re-layouts  32.5 us (5%)
  other arithmetic  24 us (4%)
  between operations  14.9 us (2%)
    psum x1, waiting for transfers between devices, body(): lax.psum((grad_query_weight, grad_query_bias, grad_key_weight, grad_value...  169 us
    reduce_scatter x1, waiting for transfers between devices, body(): lax.psum_scatter(jnp.einsum('rf,df->rd', grad_in, up_weight, preferred_el...  53.8 us
    reduce_scatter x1, waiting for transfers between devices, feedforward(): lax.psum_scatter(jnp.dot(act, down_weight, preferred_element_type=jnp.flo...  53.8 us
    reduce_scatter x1, waiting for transfers between devices, attention_forward(): lax.psum_scatter(jnp.dot(context, out_weight, preferred_element_type=jnp....  53.7 us
    psum x1, blocking collectives, body(): lax.psum((attn_gain_part, attn_shift_part, final_gain_part, final_shift_p...  41.6 us
    psum x1, blocking collectives, body(): lax.psum((grad_query_weight, grad_query_bias, grad_key_weight, grad_value...  39.6 us
    all_gather x1, waiting for transfers between devices, attention_forward(): whole = lax.all_gather(tokens, 'mp', axis=0, tiled=True)  29.3 us
    all_gather x1, waiting for transfers between devices, body(): lax.all_gather(grad_final.astype(jnp.bfloat16), 'mp', axis=0, tiled=True)  26.7 us
  transfers between devices with their start and end apart: 9, of which 8 were waited for; matrix products, arithmetic and copies ran while one was open for 4% of the time, Pallas kernels for 0%

commit v1 on v0

v1 whole, which is shorter than its diff:
```python
import functools

import jax
import jax.numpy as jnp
from jax import lax
from jax.experimental import pallas as pl
from jax.experimental.pallas import tpu as pltpu
from jax.sharding import PartitionSpec as P

HEAD = 64
MAXREG = 100
EPS = 1e-12
ROOT_HALF = 0.7071067811865476
DENSITY = 0.3989422804014327
MASKED = -1e30

D = 768
LEN = 228
MESH = pl.DeviceIdType.MESH
F32 = jnp.float32
BF16 = jnp.bfloat16


def flip(index, bit):
    return index + bit - 2 * bit * ((index // bit) % 2)


class Peers:
    def __init__(self, dp_size):
        self.dp = lax.axis_index("dp")
        self.mp = lax.axis_index("mp")
        self.core = {"dp": self.dp, "mp": flip(self.mp, 1)}
        self.across = {"dp": self.dp, "mp": flip(self.mp, 2)}
        self.pair_at = self.dp % 2
        self.pair = {"dp": flip(self.dp, 1), "mp": self.mp}
        self.line_at = (self.dp // 2) % 4
        self.line = []
        self.line_slot = []
        for step in range(1, 4):
            slot = (self.line_at + step) % 4
            self.line_slot.append(slot)
            self.line.append({"dp": self.dp + 2 * (slot - self.line_at), "mp": self.mp})
        self.extra = []
        bit = 8
        while bit < dp_size:
            self.extra.append({"dp": flip(self.dp, bit), "mp": self.mp})
            bit *= 2
        self.cube = [
            self.core,
            self.across,
            self.pair,
            {"dp": flip(self.dp, 2), "mp": self.mp},
            {"dp": flip(self.dp, 4), "mp": self.mp},
        ] + self.extra


def greet(peers):
    barrier = pltpu.get_barrier_semaphore()
    for peer in peers:
        pl.semaphore_signal(barrier, inc=1, device_id=peer, device_id_type=MESH)
    pl.semaphore_wait(barrier, len(peers))


def remote(src, dst, sems, at, peer):
    return pltpu.make_async_remote_copy(
        src_ref=src,
        dst_ref=dst,
        send_sem=sems.at[0, at],
        recv_sem=sems.at[1, at],
        device_id=peer,
        device_id_type=MESH,
    )


HALF = D // 2
GATHER_CUTS = 2
GATHER_ROWS = HALF // GATHER_CUTS


class Gather:
    def __init__(self, peers, whole, sems):
        self.peers, self.whole, self.sems = peers, whole, sems
        self.own = peers.mp
        self.far = flip(peers.mp, 2)

    def rows(self, half, cut):
        return pl.ds(pl.multiple_of(half * HALF + cut * GATHER_ROWS, GATHER_ROWS), GATHER_ROWS)

    def piece(self, shard, half, cut, at, peer):
        view = self.whole.at[shard, self.rows(half, cut), :]
        return remote(view, view, self.sems, at, peer)

    def to_core(self):
        view = self.whole.at[self.own]
        return remote(view, view, self.sems, 0, self.peers.core)

    def across(self, cut):
        return self.piece(self.own, self.peers.pair_at, cut, 1 + cut, self.peers.across)

    def to_pair(self, cut):
        return self.piece(self.far, self.peers.pair_at, cut, 1 + GATHER_CUTS + cut, self.peers.pair)

    def far_to_core(self, cut):
        return self.piece(self.far, self.peers.pair_at, cut, 1 + 2 * GATHER_CUTS + cut, self.peers.core)

    def rest_to_core(self, cut):
        return self.piece(self.far, 1 - self.peers.pair_at, cut, 1 + 3 * GATHER_CUTS + cut, self.peers.core)

    def start(self):
        for cut in range(GATHER_CUTS):
            self.across(cut).start()
        self.to_core().start()

    def relay(self, cut):
        self.across(cut).wait_recv()
        self.to_pair(cut).start()
        self.far_to_core(cut).start()

    def relay_rest(self, cut):
        self.to_pair(cut).wait_recv()
        self.rest_to_core(cut).start()

    def wait_near(self):
        self.to_core().wait_recv()

    def wait_far_core(self):
        for cut in range(GATHER_CUTS):
            self.far_to_core(cut).wait_recv()
            self.rest_to_core(cut).wait_recv()

    def drain(self):
        self.to_core().wait_send()
        for cut in range(GATHER_CUTS):
            self.across(cut).wait_send()
            self.to_pair(cut).wait_send()
            self.far_to_core(cut).wait_send()
            self.rest_to_core(cut).wait_send()


GATHER_SEMS = 1 + 4 * GATHER_CUTS


UNIT = 384
PART = UNIT // 2
PIECE = PART // 4
TILE = 48


def add_rows(into, into_at, other, other_at, rows):
    def step(i, carry):
        a = pl.ds(pl.multiple_of(into_at + i * TILE, 16), TILE)
        b = pl.ds(pl.multiple_of(other_at + i * TILE, 16), TILE)
        into[a, :] = (into[a, :].astype(F32) + other[b, :].astype(F32)).astype(BF16)
        return carry

    lax.fori_loop(0, rows // TILE, step, 0)


class Reduce:
    def __init__(self, peers, own, row0, from_core, from_across, from_pair, from_line, from_extra, final, sems):
        self.p = peers
        self.own, self.row0 = own, row0
        self.from_core, self.from_across, self.from_pair = from_core, from_across, from_pair
        self.from_line, self.from_extra, self.final, self.sems = from_line, from_extra, final, sems
        self.core_at = peers.mp % 2
        self.far = flip(peers.mp, 2)

    def view(self, shard, start, rows):
        return self.own.at[shard, pl.ds(pl.multiple_of(self.row0 + start, 16), rows), :]

    def to_core(self, x):
        shard = 2 * x + 1 - self.core_at
        return remote(self.view(shard, 0, UNIT), self.from_core.at[x], self.sems, x, self.p.core)

    def to_across(self):
        return remote(self.view(self.far, 0, UNIT), self.from_across, self.sems, 2, self.p.across)

    def to_pair(self):
        start = (1 - self.p.pair_at) * PART
        return remote(self.view(self.p.mp, start, PART), self.from_pair, self.sems, 3, self.p.pair)

    def to_line(self, step):
        start = self.p.pair_at * PART + self.p.line_slot[step] * PIECE
        return remote(
            self.view(self.p.mp, start, PIECE), self.from_line.at[step], self.sems, 4 + step, self.p.line[step]
        )

    def mine(self):
        return self.p.pair_at * PART + self.p.line_at * PIECE

    def final_view(self, start, rows):
        return self.final.at[pl.ds(pl.multiple_of(self.row0 + start, 16), rows), :]

    def back_line(self, step):
        view = self.final_view(self.mine(), PIECE)
        return remote(view, view, self.sems, 7 + step, self.p.line[step])

    def back_pair(self):
        view = self.final_view(self.p.pair_at * PART, PART)
        return remote(view, view, self.sems, 10, self.p.pair)

    def extra(self, at):
        view = self.final_view(self.mine(), PIECE)
        return remote(view, self.from_extra.at[at], self.sems, 11 + at, self.p.extra[at])

    def start(self):
        for x in range(2):
            self.to_core(x).start()

    def after_core(self):
        for step in range(2):
            x = (self.p.mp // 2 + 1 + step) % 2
            shard = 2 * x + self.core_at
            if step == 0:
                for y in range(2):
                    self.to_core(y).wait_recv()
            add_rows(self.own.at[shard], self.row0, self.from_core.at[x], 0, UNIT)
            if step == 0:
                self.to_across().start()

    def after_across(self):
        self.to_across().wait_recv()
        other = (1 - self.p.pair_at) * PART
        add_rows(self.own.at[self.p.mp], self.row0 + other, self.from_across, other, PART)
        self.to_pair().start()
        mine = self.p.pair_at * PART
        add_rows(self.own.at[self.p.mp], self.row0 + mine, self.from_across, mine, PART)

    def after_pair(self):
        self.to_pair().wait_recv()
        mine = self.p.pair_at * PART
        add_rows(self.own.at[self.p.mp], self.row0 + mine, self.from_pair, 0, PART)
        for step in range(3):
            self.to_line(step).start()

    def after_line(self):
        for step in range(3):
            self.to_line(step).wait_recv()
        at = pl.multiple_of(self.row0 + self.mine(), 16)
        total = self.own[self.p.mp, pl.ds(at, PIECE), :].astype(F32)
        for step in range(3):
            total = total + self.from_line[step].astype(F32)
        self.final[pl.ds(at, PIECE), :] = total.astype(BF16)
        for i in range(len(self.p.extra)):
            self.extra(i).start()
            self.extra(i).wait()
            add_rows(self.final, self.row0 + self.mine(), self.from_extra.at[i], 0, PIECE)
        for step in range(3):
            self.back_line(step).start()

    def after_back_line(self):
        for step in range(3):
            self.back_line(step).wait_recv()
        self.back_pair().start()

    def finish(self):
        self.back_pair().wait_recv()

    def drain(self):
        for x in range(2):
            self.to_core(x).wait_send()
        self.to_across().wait_send()
        self.to_pair().wait_send()
        self.back_pair().wait_send()
        for step in range(3):
            self.to_line(step).wait_send()
            self.back_line(step).wait_send()


REDUCE_SEMS = 11
SMALL = 16


SMALL = 16


class SmallSum:
    def __init__(self, peers, totals, boxes, line_boxes, sems):
        self.p, self.totals, self.boxes, self.line_boxes, self.sems = peers, totals, boxes, line_boxes, sems
        self.pairwise = [peers.core, peers.across, peers.pair]

    def copy(self, at):
        return remote(self.totals.at[at], self.boxes.at[at], self.sems, at, self.pairwise[at])

    def send(self, at):
        self.copy(at).start()

    def add(self, at):
        self.copy(at).wait_recv()
        self.totals[at + 1] = self.totals[at] + self.boxes[at]

    def line_copy(self, step):
        return remote(
            self.totals.at[3], self.line_boxes.at[self.p.line_at], self.sems, 3 + step, self.p.line[step]
        )

    def send_line(self):
        for step in range(3):
            self.line_copy(step).start()
        self.line_boxes[self.p.line_at] = self.totals[3]

    def add_line(self):
        for step in range(3):
            self.line_copy(step).wait_recv()
        self.totals[4] = (self.line_boxes[0] + self.line_boxes[1]) + (self.line_boxes[2] + self.line_boxes[3])
        for at in range(len(self.p.extra)):
            copy = self.extra_copy(at)
            copy.start()
            copy.wait()
            self.totals[5 + at] = self.totals[4 + at] + self.boxes[3 + at]

    def extra_copy(self, at):
        return remote(self.totals.at[4 + at], self.boxes.at[3 + at], self.sems, 6 + at, self.p.extra[at])

    def result(self):
        return self.totals.at[4 + len(self.p.extra)]

    def drain(self):
        for at in range(3):
            self.copy(at).wait_send()
        for step in range(3):
            self.line_copy(step).wait_send()


SMALL_SEMS = 6
SEQ = 256
ROWS = 2 * SEQ
HEADS_HERE = 3
PART_D = D // 4
SCALE = HEAD**-0.5


def dot(left, right, at):
    return lax.dot_general(left, right, ((at[:1], at[1:]), ((), ())), preferred_element_type=F32)


NN, NT, TN = (1, 0), (1, 1), (0, 0)


def mean(v):
    return jnp.sum(v, axis=-1, keepdims=True) * (1.0 / D)


def fold(v):
    return jnp.sum(v.reshape(v.shape[0] // 8, 8, v.shape[1]), axis=0)


def times(count, step):
    def wrapped(i, carry):
        step(i)
        return carry

    lax.fori_loop(0, count, wrapped, 0)


UNITS = 6


def layer_kernel(
    dp_size,
    x_in, c_in, mask, params, bias_in, a_in, u_in, d_in,
    out_hbm, gtok_hbm, ga_hbm, gu_hbm, gd_hbm, small_hbm,
    wa, wu, wd, bias, x, c, qkv, probs, ctx, dctx, y1, r1, mid_low, act, slope, acc, dz, tmp, dlow, out,
    sums, ub_sums, pd, fa, fu, fd,
    from_core, from_across, from_pair, from_line, from_extra,
    small_totals, small_boxes, small_line, sems, small_sems, sa, su, sd, sb, local,
):
    peers = Peers(dp_size)
    diag = {"dp": peers.dp, "mp": flip(flip(peers.mp, 1), 2)}
    me_x, me_c = peers.mp // 2, peers.mp % 2

    def shard(r):
        return 2 * ((me_x + r // 2) % 2) + (me_c + r % 2) % 2

    loads = [
        (a_in, wa.at[peers.mp]),
        (u_in, wu.at[peers.mp]),
        (d_in, wd.at[peers.mp]),
        (bias_in, bias.at[peers.mp]),
        (x_in, x),
        (c_in, c),
    ]
    loads = [pltpu.make_async_copy(src, dst, local.at[i]) for i, (src, dst) in enumerate(loads)]
    for load in (loads[0], loads[3], loads[4], loads[1], loads[2], loads[5]):
        load.start()
    greet([peers.core, peers.across, diag, peers.pair] + peers.line + peers.extra)
    bias_peers = [peers.core, peers.across, diag]
    bias_copies = [
        remote(bias.at[peers.mp], bias.at[peers.mp], sb, i, peer) for i, peer in enumerate(bias_peers)
    ]
    ga_, gu_, gd_ = (Gather(peers, w, s) for w, s in ((wa, sa), (wu, su), (wd, sd)))
    loads[3].wait()
    for copy in bias_copies:
        copy.start()
    for load, g in zip(loads[:3], (ga_, gu_, gd_)):
        load.wait()
        g.start()
    loads[4].wait()
    for copy in bias_copies:
        copy.wait()

    def project(r):
        s = shard(r)
        column = jnp.transpose(bias[s])[0 : 3 * PART_D, 0:1]
        qkv[s] = (dot(wa[s, 0 : 3 * PART_D, :], x[...], NT) + column).astype(BF16)

    def places(s, i):
        head, seq = i // 2, i % 2
        lanes = pl.ds(pl.multiple_of(seq * SEQ, SEQ), SEQ)
        return (
            seq,
            lanes,
            [pl.ds(pl.multiple_of(kind * PART_D + head * HEAD, HEAD), HEAD) for kind in range(3)],
        )

    def attend(r):
        s = shard(r)

        def step(i):
            seq, lanes, (q_at, k_at, v_at) = places(s, i)
            scores = dot(qkv[s, k_at, lanes], qkv[s, q_at, lanes], TN) * SCALE
            keep = mask[pl.ds(pl.multiple_of(seq * SEQ, SEQ), SEQ), :]
            scores = scores * keep + (keep - 1.0) * 1e30
            top = jnp.max(scores, axis=0, keepdims=True)
            weights = jnp.exp(scores - top)
            total = jnp.sum(weights, axis=0, keepdims=True)
            low = (weights * (1.0 / total)).astype(BF16)
            probs[s * 6 + i] = low
            ctx[s, q_at, lanes] = dot(qkv[s, v_at, lanes], low, NN).astype(BF16)

        times(6, step)

    project(0)
    attend(0)
    ga_.relay(0)
    ga_.wait_near()
    project(1)
    ga_.relay(1)
    attend(1)
    ga_.relay_rest(0)
    gu_.relay(0)
    ga_.relay_rest(1)
    gu_.relay(1)
    project(2)
    attend(2)
    ga_.wait_far_core()
    project(3)
    attend(3)
    gu_.relay_rest(0)
    gu_.relay_rest(1)

    wo = wa[:, 3 * PART_D :, :].reshape(D, D)
    acc[...] = dot(ctx[...].reshape(D, ROWS), wo, TN)

    RT = 32

    def rows_of(i, size):
        return pl.ds(pl.multiple_of(i * size, size), size)

    def first_norm(i):
        at = rows_of(i, RT)
        total = x[at, :].astype(F32) + acc[at, :] + params[0:1, :]
        centered = total - mean(total)
        inverse = lax.rsqrt(mean(centered * centered) + EPS)
        scaled = centered * inverse
        y1[at, :] = scaled
        r1[at, :] = jnp.broadcast_to(inverse, (RT, 128))
        mid_low[at, :] = (scaled * params[1:2, :] + params[2:3, :]).astype(BF16)

    times(ROWS // RT, first_norm)

    GT = 16
    gu_.wait_near()

    def feed(r):
        s = shard(r)
        tmp[...] = dot(mid_low[...], wu[s], NN)
        shift = bias[s, 1:2, :]

        def gelu(i):
            at = rows_of(i, GT)
            value = tmp[at, :] + shift
            cdf = 0.5 * (1.0 + lax.erf(value * ROOT_HALF))
            act[s, at, :] = (value * cdf).astype(BF16)
            slope[s, at, :] = (cdf + value * jnp.exp(-0.5 * value * value) * DENSITY).astype(BF16)

        times(ROWS // GT, gelu)

    times(2, feed)
    gd_.relay(0)
    gd_.relay(1)
    gu_.wait_far_core()
    times(2, lambda r: feed(r + 2))
    gd_.relay_rest(0)
    gd_.relay_rest(1)
    gd_.wait_near()
    acc[...] = dot(act[shard(0)], wd[shard(0)], NN)
    acc[...] += dot(act[shard(1)], wd[shard(1)], NN)
    acc[...] += dot(act[shard(2)], wd[shard(2)], NN)
    gd_.wait_far_core()
    acc[...] += dot(act[shard(3)], wd[shard(3)], NN)
    loads[5].wait()
    sums[...] = jnp.zeros_like(sums)
    ub_sums[...] = jnp.zeros_like(ub_sums)

    def second_norm(i):
        at = rows_of(i, RT)
        mid = y1[at, :] * params[1:2, :] + params[2:3, :]
        total = mid + acc[at, :] + params[3:4, :]
        centered = total - mean(total)
        inverse = lax.rsqrt(mean(centered * centered) + EPS)
        scaled = centered * inverse
        gain = params[4:5, :]
        out[at, :] = (scaled * gain + params[5:6, :]).astype(BF16)
        grad = c[at, :].astype(F32)
        weighted = grad * gain
        back = inverse * (weighted - mean(weighted) - scaled * mean(weighted * scaled))
        low = back.astype(BF16)
        dz[at, :] = back
        dlow[at, :] = low
        sums[0] += fold(grad * scaled)
        sums[1] += fold(grad)
        sums[2] += fold(low.astype(F32))

    times(ROWS // RT, second_norm)
    out_copy = pltpu.make_async_copy(out, out_hbm, local.at[6])
    out_copy.start()

    units = []
    for n in range(UNITS):
        own, final = ((pd, fd), (wd, fu), (wu, fa))[n // 2]
        units.append(
            Reduce(
                peers, own, (n % 2) * UNIT, from_core.at[n], from_across.at[n], from_pair.at[n],
                from_line.at[n], from_extra.at[n], final, sems.at[n],
            )
        )

    def down_grads(h):
        def one(r):
            s = shard(r)
            pd[s, h * UNIT : (h + 1) * UNIT, :] = dot(
                dlow[:, h * UNIT : (h + 1) * UNIT], act[s], TN
            ).astype(BF16)

        times(4, one)

    down_grads(0)
    units[0].start()
    down_grads(1)
    units[0].after_core()
    units[1].start()

    def hidden(r):
        s = shard(r)
        tmp[...] = dot(dlow[...], wd[s], NT)

        def scale(i):
            at = rows_of(i, RT)
            low = (tmp[at, :] * slope[s, at, :].astype(F32)).astype(BF16)
            slope[s, at, :] = low
            ub_sums[s] += fold(low.astype(F32))

        times(ROWS // RT, scale)

    times(4, hidden)
    units[1].after_core()
    ga_.drain()
    gu_.drain()
    gd_.drain()

    def up_grads(h):
        def one(r):
            s = shard(r)
            wd[s, h * UNIT : (h + 1) * UNIT, :] = dot(
                mid_low[:, h * UNIT : (h + 1) * UNIT], slope[s], TN
            ).astype(BF16)

        times(4, one)

    up_grads(0)
    units[2].start()
    up_grads(1)
    units[2].after_core()
    units[3].start()
    acc[...] = dot(slope[0], wu[0], NT)
    times(3, lambda r: acc.__setitem__(..., acc[...] + dot(slope[r + 1], wu[r + 1], NT)))
    units[3].after_core()

    def first_norm_back(i):
        at = rows_of(i, RT)
        grad = dz[at, :] + acc[at, :]
        scaled = y1[at, :]
        weighted = grad * params[1:2, :]
        back = r1[at, 0:1] * (weighted - mean(weighted) - scaled * mean(weighted * scaled))
        low = back.astype(BF16)
        dz[at, :] = back
        dlow[at, :] = low
        sums[3] += fold(grad * scaled)
        sums[4] += fold(grad)
        sums[5] += fold(low.astype(F32))

    times(ROWS // RT, first_norm_back)
    units[0].after_across()

    def out_grads(r):
        s = shard(r)
        wu[s, 3 * PART_D :, :] = dot(ctx[s], dlow[...], NN).astype(BF16)
        dctx[s] = dot(wa[s, 3 * PART_D :, :], dlow[...], NT).astype(BF16)

    times(4, out_grads)

    def attend_back(r):
        s = shard(r)

        def step(i):
            seq, lanes, (q_at, k_at, v_at) = places(s, i)
            low = probs[s * 6 + i]
            query, key, value = (qkv[s, at, lanes] for at in (q_at, k_at, v_at))
            grad = dctx[s, q_at, lanes]
            grad_value = dot(grad, low, NT).astype(BF16)
            grad_probs = dot(value, grad, TN)
            wide = low.astype(F32)
            row_total = jnp.sum(wide * grad_probs, axis=0, keepdims=True)
            grad_scores = (wide * (grad_probs - row_total)).astype(BF16)
            qkv[s, q_at, lanes] = (dot(key, grad_scores, NN) * SCALE).astype(BF16)
            qkv[s, k_at, lanes] = (dot(query, grad_scores, NT) * SCALE).astype(BF16)
            qkv[s, v_at, lanes] = grad_value

        times(6, step)

    times(2, attend_back)
    units[0].after_pair()
    units[1].after_across()
    times(2, lambda r: attend_back(r + 2))
    units[0].after_line()
    units[1].after_pair()

    def in_grads(start, rows):
        def one(r):
            s = shard(r)
            wu[s, start : start + rows, :] = dot(qkv[s, start : start + rows, :], x[...], NN).astype(BF16)

        times(4, one)

    in_grads(0, UNIT)
    units[4].start()
    in_grads(UNIT, PART_D)
    units[4].after_core()
    units[5].start()
    small = SmallSum(peers, small_totals, small_boxes, small_line, small_sems)
    ones = jnp.ones((16, ROWS), BF16)

    def pack(r):
        s = shard(r)
        column_sums = dot(ones, qkv[s], NT)
        small_totals[0, pl.ds(s, 1), 0 : 3 * PART_D] = column_sums[0:1, :]
        small_totals[0, pl.ds(s, 1), 3 * PART_D :] = jnp.zeros((1, PART_D), F32)
        small_totals[0, pl.ds(4 + s, 1), :] = jnp.sum(ub_sums[s], axis=0, keepdims=True)

    times(4, pack)
    for i in range(6):
        small_totals[0, 8 + i : 9 + i, :] = jnp.sum(sums[i], axis=0, keepdims=True)
    small_totals[0, 14:16, :] = jnp.zeros((2, D), F32)
    small.send(0)
    units[5].after_core()
    small.add(0)
    small.send(1)

    def token_grads(r):
        s = shard(r)
        dz[...] += dot(qkv[s], wa[s, 0 : 3 * PART_D, :], TN)

    stages = ("after_across", "after_pair", "after_line", "after_back_line", "finish")
    done = [3, 2, 0, 0, 0, 0]
    times(4, token_grads)
    gtok_copy = pltpu.make_async_copy(dz, gtok_hbm, local.at[7])
    gtok_copy.start()
    finals, outs = (fd, fu, fa), (gd_hbm, gu_hbm, ga_hbm)

    def run(n, stage):
        assert done[n] == stage, (n, stage, done)
        done[n] = stage + 1
        getattr(units[n], stages[stage])()
        if n == UNITS - 1:
            if stage == 0:
                small.add(1)
                small.send(2)
            elif stage == 1:
                small.add(2)
                small.send_line()
            elif stage == 2:
                small.add_line()
        if stage == 4 and n % 2 == 1:
            pltpu.make_async_copy(finals[n // 2], outs[n // 2], local.at[8 + n // 2]).start()

    run(2, 0)
    for tick in range(3, UNITS + 4):
        for stage in reversed(range(5)):
            n = tick - stage
            if 0 <= n < UNITS and done[n] == stage:
                run(n, stage)
    for n in range(UNITS):
        while done[n] < 5:
            run(n, done[n])
    small_copy = pltpu.make_async_copy(small.result(), small_hbm, local.at[11])
    small_copy.start()
    for unit in units:
        unit.drain()
    small.drain()
    out_copy.wait()
    gtok_copy.wait()
    for t in range(3):
        pltpu.make_async_copy(finals[t], outs[t], local.at[8 + t]).wait()
    small_copy.wait()


def extras_of(dp_size):
    count, bit = 0, 8
    while bit < dp_size:
        count, bit = count + 1, bit * 2
    return count


def layer(dp_size, x, c, mask, params, bias, a, u, d):
    extras = extras_of(dp_size)
    block = jax.ShapeDtypeStruct((D, D), BF16)
    anywhere = pl.BlockSpec(memory_space=pl.ANY)
    vmem = pl.BlockSpec(memory_space=pltpu.VMEM)
    whole = pltpu.VMEM((4, D, D), BF16)
    low = pltpu.VMEM((ROWS, D), BF16)
    wide = pltpu.VMEM((ROWS, D), F32)
    hidden = pltpu.VMEM((4, ROWS, D), BF16)
    final = pltpu.VMEM((D, D), BF16)
    scratch = dict(
        wa=whole, wu=whole, wd=whole, bias=pltpu.VMEM((4, 8, D), F32), x=low, c=low,
        qkv=pltpu.VMEM((4, 3 * PART_D, ROWS), BF16),
        probs=pltpu.VMEM((24, SEQ, SEQ), BF16),
        ctx=pltpu.VMEM((4, PART_D, ROWS), BF16),
        dctx=pltpu.VMEM((4, PART_D, ROWS), BF16),
        y1=wide, r1=pltpu.VMEM((ROWS, 128), F32), mid_low=low, act=hidden, slope=hidden,
        acc=wide, dz=wide, tmp=wide, dlow=low, out=low,
        sums=pltpu.VMEM((6, 8, D), F32), ub_sums=pltpu.VMEM((4, 8, D), F32), pd=whole,
        fa=final, fu=final, fd=final,
        from_core=pltpu.VMEM((UNITS, 2, UNIT, D), BF16),
        from_across=pltpu.VMEM((UNITS, UNIT, D), BF16),
        from_pair=pltpu.VMEM((UNITS, PART, D), BF16),
        from_line=pltpu.VMEM((UNITS, 3, PIECE, D), BF16),
        from_extra=pltpu.VMEM((UNITS, max(extras, 1), PIECE, D), BF16),
        small_totals=pltpu.VMEM((5 + extras, SMALL, D), F32),
        small_boxes=pltpu.VMEM((3 + extras, SMALL, D), F32),
        small_line=pltpu.VMEM((4, SMALL, D), F32),
        sems=pltpu.SemaphoreType.DMA((UNITS, 2, REDUCE_SEMS + extras)),
        small_sems=pltpu.SemaphoreType.DMA((2, SMALL_SEMS + extras)),
        sa=pltpu.SemaphoreType.DMA((2, GATHER_SEMS)),
        su=pltpu.SemaphoreType.DMA((2, GATHER_SEMS)),
        sd=pltpu.SemaphoreType.DMA((2, GATHER_SEMS)),
        sb=pltpu.SemaphoreType.DMA((2, 3)),
        local=pltpu.SemaphoreType.DMA((12,)),
    )
    return pl.pallas_call(
        functools.partial(layer_kernel, dp_size),
        out_shape=(
            jax.ShapeDtypeStruct((ROWS, D), BF16),
            jax.ShapeDtypeStruct((ROWS, D), F32),
            block,
            block,
            block,
            jax.ShapeDtypeStruct((SMALL, D), F32),
        ),
        in_specs=[anywhere, anywhere, vmem, vmem, anywhere, anywhere, anywhere, anywhere],
        out_specs=(anywhere,) * 6,
        scratch_shapes=list(scratch.values()),
        compiler_params=pltpu.CompilerParams(
            collective_id=0, has_side_effects=True, vmem_limit_bytes=67043328
        ),
    )(x, c, mask, params, bias, a, u, d)


def key_valid(caption_mask, region_counts, group_ids):
    images = region_counts.shape[0]
    match = group_ids[:, None] == jnp.arange(images, dtype=jnp.int32)[None, :]
    regions = jnp.sum(jnp.where(match, region_counts[None, :], 0), axis=1)
    slots = jnp.arange(MAXREG, dtype=jnp.int32)
    return jnp.concatenate([caption_mask > 0, slots[None, :] < regions[:, None]], axis=1)


def body(
    dp_size,
    tokens,
    caption_mask,
    region_counts,
    group_ids,
    query_weight,
    query_bias,
    key_weight,
    value_weight,
    value_bias,
    out_weight,
    out_bias,
    attn_gain,
    attn_shift,
    up_weight,
    up_bias,
    down_weight,
    down_bias,
    final_gain,
    final_shift,
    cotangent,
):
    mp = lax.axis_index("mp")
    seqs = tokens.shape[0] // LEN
    valid = lax.dynamic_slice_in_dim(
        key_valid(caption_mask, region_counts, group_ids), mp * seqs, seqs, 0
    )
    attn_block = jnp.concatenate([query_weight.T, key_weight.T, value_weight.T, out_weight], axis=0)
    part = D // 4
    zeros = jnp.zeros((part,), F32)
    bias = jnp.concatenate(
        [
            jnp.concatenate([query_bias, zeros, value_bias, zeros])[None],
            up_bias[None],
            jnp.zeros((6, D), F32),
        ],
        axis=0,
    )
    params = jnp.stack(
        [out_bias, attn_gain, attn_shift, down_bias, final_gain, final_shift] + [jnp.zeros((D,), F32)] * 2
    )
    fill = ((0, 0), (0, SEQ - LEN), (0, 0))
    spread = lambda v: jnp.pad(v.reshape(seqs, LEN, D), fill).reshape(ROWS, D)
    mask = jnp.pad(valid.astype(F32), fill[:2]).reshape(ROWS, 1)
    out, grad_tokens, ga, gu, gd, small = layer(
        dp_size, spread(tokens), spread(cotangent), mask, params, bias, attn_block, up_weight, down_weight
    )
    trim = lambda v: v.reshape(seqs, SEQ, D)[:, :LEN].reshape(seqs * LEN, D)
    ga = ga.astype(F32)
    mine = lax.dynamic_index_in_dim(small, mp, 0, keepdims=False)
    return (
        trim(out),
        trim(grad_tokens),
        ga[:part].T,
        mine[:part],
        ga[part : 2 * part].T,
        ga[2 * part : 3 * part].T,
        mine[2 * part : 3 * part],
        ga[3 * part :],
        small[13],
        small[11],
        small[12],
        gu.astype(F32),
        lax.dynamic_index_in_dim(small, 4 + mp, 0, keepdims=False),
        gd.astype(F32).T,
        small[10],
        small[8],
        small[9],
    )


def solution(mesh):
    return jax.shard_map(
        functools.partial(body, mesh.shape["dp"]),
        mesh=mesh,
        in_specs=(
            P(("dp", "mp"), None),
            P("dp", None),
            P(),
            P("dp"),
            P(None, "mp"),
            P("mp"),
            P(None, "mp"),
            P(None, "mp"),
            P("mp"),
            P("mp", None),
            P(),
            P(),
            P(),
            P(None, "mp"),
            P("mp"),
            P("mp", None),
            P(),
            P(),
            P(),
            P(("dp", "mp"), None),
        ),
        out_specs=(
            P(("dp", "mp"), None),
            P(("dp", "mp"), None),
            P(None, "mp"),
            P("mp"),
            P(None, "mp"),
            P(None, "mp"),
            P("mp"),
            P("mp", None),
            P(),
            P(),
            P(),
            P(None, "mp"),
            P("mp"),
            P("mp", None),
            P(),
            P(),
            P(),
        ),
        check_vma=False,
    )
```

time: 678 us -> 219 us (0.32); the launches traced: 670 us -> 219 us
  waiting for transfers between devices: 440 us -> 0 us
  Pallas kernels: 0 us -> 194 us
  blocking collectives: 81.2 us -> 0 us
  matrix products: 76.6 us -> 0 us
  other arithmetic: 24 us -> 6.67 us
  local copies, waits for them, and re-layouts: 32.5 us -> 17.1 us
  between operations: 14.9 us -> 0.93 us
    pallas_call x0 -> x1, Pallas kernels: none -> 194 us  [layer(): pl.pallas_call(functools.partial(layer_kernel, dp_size), out_shape=(jax.S...]
    psum x1 -> x0, waiting for transfers between devices: 169 us -> none  [body(): lax.psum((grad_query_weight, grad_query_bias, grad_key_weight, grad_value...]
    reduce_scatter x4 -> x0, waiting for transfers between devices: 161 us -> none  [the longest x1 53.8 us: body(): lax.psum_scatter(jnp.einsum('rf,df->rd', grad_in, up_weight, preferred_el...]
    all_gather x4 -> x0, waiting for transfers between devices: 109 us -> none  [the longest x1 29.3 us: attention_forward(): whole = lax.all_gather(tokens, 'mp', axis=0, tiled=True)]
    psum x2 -> x0, blocking collectives: 81.2 us -> none  [the longest x1 41.6 us: body(): lax.psum((attn_gain_part, attn_shift_part, final_gain_part, final_shift_p...]
    dot_general x24 -> x0, matrix products: 76.6 us -> none  [the longest x1 6.86 us: body(): jnp.einsum('rf,rd->fd', act, grad_branch, preferred_element_type=jnp.floa...]
    reduce_sum x9 -> x0, other arithmetic: 14.4 us -> none  [the longest x1 3.78 us: body(): attn_gain_part = jnp.sum(grad_mid * scaled_mid, axis=0)]
    unnamed x94 -> x39, local copies, waits for them, and re-layouts: 15.2 us -> 4.22 us
  transfers between devices with their start and end apart: 9 -> 0, of which waited for: 8 -> 0; matrix products, arithmetic and copies ran while one was open for 4% -> 0% of each run, Pallas kernels for 0% -> 0%
where the time goes in v1:
time: 219 us
  Pallas kernels  194 us (89%)
  local copies, waits for them, and re-layouts  17.1 us (8%)
  other arithmetic  6.67 us (3%)
    pallas_call x1, Pallas kernels, layer(): pl.pallas_call(functools.partial(layer_kernel, dp_size), out_shape=(jax.S...  194 us

profile of v1, /device:TPU:0, one launch (start us, length us, event | category | flops | bytes accessed | tf_op | source)
XLA Modules:
  0.0 218.6 jit_solution(11008480645160637139)
XLA Ops:
  0.7 0.9 select_reduce_fusion
  1.6 0.7 broadcast_compare_fusion
  2.3 0.9 copy.43
  3.2 1.2 reshape.68
  4.4 0.9 pad.12
  5.6 0.9 pad.13
  6.6 0.2 copy-done.8
  6.7 1.1 pad_maximum_fusion.a_in
  8.0 0.6 stack.31.params
  8.8 0.7 maximum_maximum_fusion.bias_in
  9.5 193.9 %shard_map.323 = (bf16[512,768]{1,0:T(8,128)(2,1)}, f32[512,768]{1,0:T(8,128)}, bf16[768,768]{1,0:T(8,128)(2,1)}, bf16[768,768]{1,0:T(8,128)(2,1)}, bf16[768,768]{1,0:T(8,128)(2,1)}, /*index=5*/f32[16,768]{1,0:T(8,128)}) custom-call(bf16[512,768]{1,0:T(8,128)(2,1)} %bitcast.22, bf16[512,768]{1,0:T(8,128)(2,1)} %bitcast.23, f32[512,1]{1,0:T(8,128)} %bitcast.25, ...), custom_call_target="tpu_custom_call" | custom-call | tf_op jit(solution)/shard_map/pallas_call | solution.py:761
  203.4 1.8 slice_reduce_fusion
  205.1 1.4 fusion.2
  206.5 1.4 convert_element_type.13
  207.9 1.2 slice_bitcast_fusion
  209.2 0.6 copy-done
  209.8 0.9 slice.69
  210.7 0.2 convert_bitcast_fusion
  210.9 2.0 copy.41
  212.8 1.4 slice.65
  214.3 1.2 reshape.77
  215.5 0.5 copy-done.1
  216.0 1.6 convert_element_type.14
  217.7 1.0 reshape.75
  (52 shorter events, 0.6 us)
Async XLA Ops:
  2.3 3.1 %copy-start.3 = (bf16[456,768]{1,0:T(8,128)(2,1)S(1)}, bf16[456,768]{1,0:T(8,128)(2,1)}, u32[]{:S(2)}) copy-start(bf16[456,768]{1,0:T(8,128)(2,1)} %param.39) | copy-start | bytes 2101252
  5.4 1.2 copy-start.5
  5.4 1.2 copy-start.6
  5.4 1.2 copy-start.7
  5.4 1.4 copy-start.8
  5.5 2.3 %copy-start.9 = (f32[768]{0:T(1024)S(1)}, f32[768]{0:T(1024)}, u32[]{:S(2)}) copy-start(f32[768]{0:T(1024)} %param.30) | copy-start | bytes 9220
  5.5 2.3 %copy-start.10 = (f32[768]{0:T(1024)S(1)}, f32[768]{0:T(1024)}, u32[]{:S(2)}) copy-start(f32[768]{0:T(1024)} %param.31) | copy-start | bytes 9220
  5.6 2.3 %copy-start.11 = (f32[768]{0:T(1024)S(1)}, f32[768]{0:T(1024)}, u32[]{:S(2)}) copy-start(f32[768]{0:T(1024)} %param.32) | copy-start | bytes 9220
  5.6 2.3 %copy-start.12 = (f32[768]{0:T(1024)S(1)}, f32[768]{0:T(1024)}, u32[]{:S(2)}) copy-start(f32[768]{0:T(1024)} %param.36) | copy-start | bytes 9220
  5.6 2.3 %copy-start.13 = (f32[768]{0:T(1024)S(1)}, f32[768]{0:T(1024)}, u32[]{:S(2)}) copy-start(f32[768]{0:T(1024)} %param.37) | copy-start | bytes 9220
  6.5 1.4 copy-start.14
  6.5 2.1 copy-start.16
  6.5 2.1 copy-start.17
  6.5 2.2 copy-start.15
  207.9 1.9 copy-start
  207.9 2.8 %copy-start.2 = (bf16[768,768]{1,0:T(8,128)(2,1)S(1)}, bf16[768,768]{1,0:T(8,128)(2,1)}, u32[]{:S(2)}) copy-start(bf16[768,768]{1,0:T(8,128)(2,1)} %get-tuple-element.28) | copy-start | bytes 3538948
  214.3 1.7 copy-start.1
  216.0 1.6 copy-start.4

commit v2 on v1

--- a/solution.py
+++ b/solution.py
@@ -1,4 +1,5 @@
 import functools
+import heapq
 
 import jax
 import jax.numpy as jnp
@@ -34,6 +35,7 @@
         self.pair_at = self.dp % 2
         self.pair = {"dp": flip(self.dp, 1), "mp": self.mp}
         self.line_at = (self.dp // 2) % 4
+        self.next = {"dp": flip(self.dp, 2), "mp": self.mp}
         self.line = []
         self.line_slot = []
         for step in range(1, 4):
@@ -72,9 +74,8 @@
     )
 
 
-HALF = D // 2
-GATHER_CUTS = 2
-GATHER_ROWS = HALF // GATHER_CUTS
+QUARTER = D // 4
+THIRD = QUARTER // 3
 
 
 class Gather:
@@ -83,83 +84,110 @@
         self.own = peers.mp
         self.far = flip(peers.mp, 2)
 
-    def rows(self, half, cut):
-        return pl.ds(pl.multiple_of(half * HALF + cut * GATHER_ROWS, GATHER_ROWS), GATHER_ROWS)
-
-    def piece(self, shard, half, cut, at, peer):
-        view = self.whole.at[shard, self.rows(half, cut), :]
+    def piece(self, shard, pair, step, start, rows, at, peer):
+        p = (self.peers.pair_at + pair) % 2
+        q = (self.peers.line_at + step) % 2
+        first = pl.multiple_of((2 * q + p) * QUARTER + start, THIRD)
+        view = self.whole.at[shard, pl.ds(first, rows), :]
         return remote(view, view, self.sems, at, peer)
 
     def to_core(self):
         view = self.whole.at[self.own]
         return remote(view, view, self.sems, 0, self.peers.core)
 
-    def across(self, cut):
-        return self.piece(self.own, self.peers.pair_at, cut, 1 + cut, self.peers.across)
-
-    def to_pair(self, cut):
-        return self.piece(self.far, self.peers.pair_at, cut, 1 + GATHER_CUTS + cut, self.peers.pair)
-
-    def far_to_core(self, cut):
-        return self.piece(self.far, self.peers.pair_at, cut, 1 + 2 * GATHER_CUTS + cut, self.peers.core)
-
-    def rest_to_core(self, cut):
-        return self.piece(self.far, 1 - self.peers.pair_at, cut, 1 + 3 * GATHER_CUTS + cut, self.peers.core)
+    def across(self):
+        return self.piece(self.own, 0, 0, 0, QUARTER, 1, self.peers.across)
+
+    def across_rest(self):
+        return self.piece(self.own, 1, 1, 0, THIRD, 2, self.peers.across)
+
+    def to_pair(self):
+        return self.piece(self.far, 0, 0, 0, QUARTER, 3, self.peers.pair)
+
+    def to_next(self):
+        return self.piece(self.far, 0, 0, 0, QUARTER, 4, self.peers.next)
+
+    def relay_next(self):
+        return self.piece(self.far, 1, 0, THIRD, THIRD, 5, self.peers.next)
+
+    def relay_pair(self):
+        return self.piece(self.far, 0, 1, 2 * THIRD, THIRD, 6, self.peers.pair)
+
+    def far_to_core(self, at):
+        return self.piece(self.far, at % 2, at // 2, 0, QUARTER, 7 + at, self.peers.core)
 
     def start(self):
-        for cut in range(GATHER_CUTS):
-            self.across(cut).start()
+        self.across().start()
+        self.across_rest().start()
         self.to_core().start()
 
-    def relay(self, cut):
-        self.across(cut).wait_recv()
-        self.to_pair(cut).start()
-        self.far_to_core(cut).start()
-
-    def relay_rest(self, cut):
-        self.to_pair(cut).wait_recv()
-        self.rest_to_core(cut).start()
+    def step1(self):
+        self.across().wait_recv()
+        self.to_pair().start()
+        self.to_next().start()
+        self.far_to_core(0).start()
+
+    def step2(self):
+        self.to_pair().wait_recv()
+        self.relay_next().start()
+        self.far_to_core(1).start()
+        self.to_next().wait_recv()
+        self.relay_pair().start()
+        self.far_to_core(2).start()
+
+    def step3(self):
+        self.across_rest().wait_recv()
+        self.relay_next().wait_recv()
+        self.relay_pair().wait_recv()
+        self.far_to_core(3).start()
 
     def wait_near(self):
         self.to_core().wait_recv()
 
     def wait_far_core(self):
-        for cut in range(GATHER_CUTS):
-            self.far_to_core(cut).wait_recv()
-            self.rest_to_core(cut).wait_recv()
+        for at in range(4):
+            self.far_to_core(at).wait_recv()
 
     def drain(self):
-        self.to_core().wait_send()
-        for cut in range(GATHER_CUTS):
-            self.across(cut).wait_send()
-            self.to_pair(cut).wait_send()
-            self.far_to_core(cut).wait_send()
-            self.rest_to_core(cut).wait_send()
-
-
-GATHER_SEMS = 1 + 4 * GATHER_CUTS
-
-
-UNIT = 384
-PART = UNIT // 2
-PIECE = PART // 4
-TILE = 48
+        for copy in (
+            self.to_core(),
+            self.across(),
+            self.across_rest(),
+            self.to_pair(),
+            self.to_next(),
+            self.relay_next(),
+            self.relay_pair(),
+        ):
+            copy.wait_send()
+        for at in range(4):
+            self.far_to_core(at).wait_send()
+
+
+GATHER_SEMS = 11
+
+
+DOWN, UP, ATTN = range(3)
+ROWS_UNIT = 128
+UNITS = tuple((weight, start) for weight in range(3) for start in range(0, D, ROWS_UNIT))
 
 
 def add_rows(into, into_at, other, other_at, rows):
+    tile = next(t for t in (64, 48, 32, 16) if rows % t == 0)
+
     def step(i, carry):
-        a = pl.ds(pl.multiple_of(into_at + i * TILE, 16), TILE)
-        b = pl.ds(pl.multiple_of(other_at + i * TILE, 16), TILE)
+        a = pl.ds(pl.multiple_of(into_at + i * tile, 16), tile)
+        b = pl.ds(pl.multiple_of(other_at + i * tile, 16), tile)
         into[a, :] = (into[a, :].astype(F32) + other[b, :].astype(F32)).astype(BF16)
         return carry
 
-    lax.fori_loop(0, rows // TILE, step, 0)
+    lax.fori_loop(0, rows // tile, step, 0)
 
 
 class Reduce:
-    def __init__(self, peers, own, row0, from_core, from_across, from_pair, from_line, from_extra, final, sems):
+    def __init__(self, peers, own, row0, rows, from_core, from_across, from_pair, from_line, from_extra, final, sems):
         self.p = peers
-        self.own, self.row0 = own, row0
+        self.own, self.row0, self.rows = own, row0, rows
+        self.part, self.piece = rows // 2, rows // 8
         self.from_core, self.from_across, self.from_pair = from_core, from_across, from_pair
         self.from_line, self.from_extra, self.final, self.sems = from_line, from_extra, final, sems
         self.core_at = peers.mp % 2
@@ -170,66 +198,67 @@
 
     def to_core(self, x):
         shard = 2 * x + 1 - self.core_at
-        return remote(self.view(shard, 0, UNIT), self.from_core.at[x], self.sems, x, self.p.core)
+        return remote(self.view(shard, 0, self.rows), self.from_core.at[x], self.sems, x, self.p.core)
 
     def to_across(self):
-        return remote(self.view(self.far, 0, UNIT), self.from_across, self.sems, 2, self.p.across)
+        return remote(self.view(self.far, 0, self.rows), self.from_across, self.sems, 2, self.p.across)
 
     def to_pair(self):
-        start = (1 - self.p.pair_at) * PART
-        return remote(self.view(self.p.mp, start, PART), self.from_pair, self.sems, 3, self.p.pair)
+        start = (1 - self.p.pair_at) * self.part
+        return remote(self.view(self.p.mp, start, self.part), self.from_pair, self.sems, 3, self.p.pair)
 
     def to_line(self, step):
-        start = self.p.pair_at * PART + self.p.line_slot[step] * PIECE
+        start = self.p.pair_at * self.part + self.p.line_slot[step] * self.piece
         return remote(
-            self.view(self.p.mp, start, PIECE), self.from_line.at[step], self.sems, 4 + step, self.p.line[step]
+            self.view(self.p.mp, start, self.piece), self.from_line.at[step], self.sems, 4 + step, self.p.line[step]
         )
 
     def mine(self):
-        return self.p.pair_at * PART + self.p.line_at * PIECE
+        return self.p.pair_at * self.part + self.p.line_at * self.piece
 
     def final_view(self, start, rows):
         return self.final.at[pl.ds(pl.multiple_of(self.row0 + start, 16), rows), :]
 
     def back_line(self, step):
-        view = self.final_view(self.mine(), PIECE)
+        view = self.final_view(self.mine(), self.piece)
         return remote(view, view, self.sems, 7 + step, self.p.line[step])
 
     def back_pair(self):
-        view = self.final_view(self.p.pair_at * PART, PART)
+        view = self.final_view(self.p.pair_at * self.part, self.part)
         return remote(view, view, self.sems, 10, self.p.pair)
 
     def extra(self, at):
-        view = self.final_view(self.mine(), PIECE)
+        view = self.final_view(self.mine(), self.piece)
         return remote(view, self.from_extra.at[at], self.sems, 11 + at, self.p.extra[at])
 
     def start(self):
         for x in range(2):
             self.to_core(x).start()
 
-    def after_core(self):
+    def after_core(self, then):
         for step in range(2):
             x = (self.p.mp // 2 + 1 + step) % 2
             shard = 2 * x + self.core_at
             if step == 0:
                 for y in range(2):
                     self.to_core(y).wait_recv()
-            add_rows(self.own.at[shard], self.row0, self.from_core.at[x], 0, UNIT)
+            add_rows(self.own.at[shard], self.row0, self.from_core.at[x], 0, self.rows)
             if step == 0:
                 self.to_across().start()
+                then()
 
     def after_across(self):
         self.to_across().wait_recv()
-        other = (1 - self.p.pair_at) * PART
-        add_rows(self.own.at[self.p.mp], self.row0 + other, self.from_across, other, PART)
+        other = (1 - self.p.pair_at) * self.part
+        add_rows(self.own.at[self.p.mp], self.row0 + other, self.from_across, other, self.part)
         self.to_pair().start()
-        mine = self.p.pair_at * PART
-        add_rows(self.own.at[self.p.mp], self.row0 + mine, self.from_across, mine, PART)
+        mine = self.p.pair_at * self.part
+        add_rows(self.own.at[self.p.mp], self.row0 + mine, self.from_across, mine, self.part)
 
     def after_pair(self):
         self.to_pair().wait_recv()
-        mine = self.p.pair_at * PART
-        add_rows(self.own.at[self.p.mp], self.row0 + mine, self.from_pair, 0, PART)
+        mine = self.p.pair_at * self.part
+        add_rows(self.own.at[self.p.mp], self.row0 + mine, self.from_pair, 0, self.part)
         for step in range(3):
             self.to_line(step).start()
 
@@ -237,14 +266,14 @@
         for step in range(3):
             self.to_line(step).wait_recv()
         at = pl.multiple_of(self.row0 + self.mine(), 16)
-        total = self.own[self.p.mp, pl.ds(at, PIECE), :].astype(F32)
+        total = self.own[self.p.mp, pl.ds(at, self.piece), :].astype(F32)
         for step in range(3):
             total = total + self.from_line[step].astype(F32)
-        self.final[pl.ds(at, PIECE), :] = total.astype(BF16)
+        self.final[pl.ds(at, self.piece), :] = total.astype(BF16)
         for i in range(len(self.p.extra)):
             self.extra(i).start()
             self.extra(i).wait()
-            add_rows(self.final, self.row0 + self.mine(), self.from_extra.at[i], 0, PIECE)
+            add_rows(self.final, self.row0 + self.mine(), self.from_extra.at[i], 0, self.piece)
         for step in range(3):
             self.back_line(step).start()
 
@@ -353,7 +382,36 @@
     lax.fori_loop(0, count, wrapped, 0)
 
 
-UNITS = 6
+class Flow:
+    UNIT_US = {"core": 1.1, "across": 4.8, "pair": 2.4, "line": 2.4}
+    WAY = ("core", "across", "pair", "line", "line", "pair")
+
+    def __init__(self, run):
+        self.run = run
+        self.now = 0.0
+        self.free = dict.fromkeys(self.UNIT_US, 0.0)
+        self.events = []
+
+    def send(self, n, stage):
+        way = self.WAY[stage]
+        self.free[way] = max(self.free[way], self.now) + self.UNIT_US[way]
+        heapq.heappush(self.events, (self.free[way] + (1.0 if way == "core" else 3.0), n, stage))
+
+    def one(self):
+        at, n, stage = heapq.heappop(self.events)
+        self.now = max(self.now, at)
+        self.run(n, stage)
+        if stage < 5:
+            self.send(n, stage + 1)
+
+    def after(self, us):
+        self.now += 1.3 * us
+        while self.events and self.events[0][0] <= self.now:
+            self.one()
+
+    def rest(self):
+        while self.events:
+            self.one()
 
 
 def layer_kernel(
@@ -432,22 +490,20 @@
 
     project(0)
     attend(0)
-    ga_.relay(0)
+    ga_.step1()
     ga_.wait_near()
     project(1)
-    ga_.relay(1)
     attend(1)
-    ga_.relay_rest(0)
-    gu_.relay(0)
-    ga_.relay_rest(1)
-    gu_.relay(1)
+    ga_.step2()
+    gu_.step1()
+    ga_.step3()
     project(2)
     attend(2)
     ga_.wait_far_core()
     project(3)
     attend(3)
-    gu_.relay_rest(0)
-    gu_.relay_rest(1)
+    gu_.step2()
+    gd_.step1()
 
     wo = wa[:, 3 * PART_D :, :].reshape(D, D)
     acc[...] = dot(ctx[...].reshape(D, ROWS), wo, TN)
@@ -468,6 +524,7 @@
         mid_low[at, :] = (scaled * params[1:2, :] + params[2:3, :]).astype(BF16)
 
     times(ROWS // RT, first_norm)
+    gu_.step3()
 
     GT = 16
     gu_.wait_near()
@@ -487,12 +544,11 @@
         times(ROWS // GT, gelu)
 
     times(2, feed)
-    gd_.relay(0)
-    gd_.relay(1)
+    gd_.step2()
+    feed(2)
+    gd_.step3()
     gu_.wait_far_core()
-    times(2, lambda r: feed(r + 2))
-    gd_.relay_rest(0)
-    gd_.relay_rest(1)
+    feed(3)
     gd_.wait_near()
     acc[...] = dot(act[shard(0)], wd[shard(0)], NN)
     acc[...] += dot(act[shard(1)], wd[shard(1)], NN)
@@ -527,29 +583,73 @@
     out_copy.start()
 
     units = []
-    for n in range(UNITS):
-        own, final = ((pd, fd), (wd, fu), (wu, fa))[n // 2]
+    for n, (weight, start) in enumerate(UNITS):
+        own, final = ((pd, fd), (wd, fu), (wu, fa))[weight]
+        row, rows = n * ROWS_UNIT, ROWS_UNIT
         units.append(
             Reduce(
-                peers, own, (n % 2) * UNIT, from_core.at[n], from_across.at[n], from_pair.at[n],
-                from_line.at[n], from_extra.at[n], final, sems.at[n],
+                peers, own, start, rows,
+                from_core.at[:, pl.ds(row, rows), :],
+                from_across.at[pl.ds(row, rows), :],
+                from_pair.at[pl.ds(row // 2, rows // 2), :],
+                from_line.at[:, pl.ds(row // 8, rows // 8), :],
+                from_extra.at[:, pl.ds(row // 8, rows // 8), :],
+                final, sems.at[n],
             )
         )
-
-    def down_grads(h):
+    small = SmallSum(peers, small_totals, small_boxes, small_line, small_sems)
+    finals, outs = (fd, fu, fa), (gd_hbm, gu_hbm, ga_hbm)
+    last = len(UNITS) - 1
+    left = [D // ROWS_UNIT] * 3
+
+    def small_after_core():
+        small.add(0)
+        small.send(1)
+
+    def run(n, stage):
+        unit = units[n]
+        if stage == 0:
+            unit.after_core(small_after_core if n == last else lambda: None)
+            return
+        (unit.after_across, unit.after_pair, unit.after_line, unit.after_back_line, unit.finish)[stage - 1]()
+        if n == last and stage == 1:
+            small.add(1)
+            small.send(2)
+        if n == last and stage == 2:
+            small.add(2)
+            small.send_line()
+        if n == last and stage == 3:
+            small.add_line()
+        if stage == 5:
+            weight = UNITS[n][0]
+            left[weight] -= 1
+            if left[weight] == 0:
+                pltpu.make_async_copy(finals[weight], outs[weight], local.at[8 + weight]).start()
+
+    flow = Flow(run)
+
+    def start(weight, row, rows):
+        for n, (other, at) in enumerate(UNITS):
+            if other == weight and row <= at < row + rows:
+                units[n].start()
+                flow.send(n, 0)
+
+    def down_grads(row, rows):
+        at = pl.ds(row, rows)
+
         def one(r):
             s = shard(r)
-            pd[s, h * UNIT : (h + 1) * UNIT, :] = dot(
-                dlow[:, h * UNIT : (h + 1) * UNIT], act[s], TN
-            ).astype(BF16)
+            pd[s, at, :] = dot(dlow[:, at], act[s], TN).astype(BF16)
 
         times(4, one)
-
-    down_grads(0)
-    units[0].start()
-    down_grads(1)
-    units[0].after_core()
-    units[1].start()
+        start(DOWN, row, rows)
+
+    down_grads(0, 128)
+    flow.after(2.0)
+    down_grads(128, 256)
+    flow.after(2.5)
+    down_grads(384, 384)
+    flow.after(0.0)
 
     def hidden(r):
         s = shard(r)
@@ -563,29 +663,31 @@
 
         times(ROWS // RT, scale)
 
-    times(4, hidden)
-    units[1].after_core()
+    times(2, hidden)
+    flow.after(2.9)
+    times(2, lambda r: hidden(r + 2))
+    flow.after(2.9)
     ga_.drain()
     gu_.drain()
     gd_.drain()
 
-    def up_grads(h):
+    def up_grads(row, rows):
+        at = pl.ds(row, rows)
+
         def one(r):
             s = shard(r)
-            wd[s, h * UNIT : (h + 1) * UNIT, :] = dot(
-                mid_low[:, h * UNIT : (h + 1) * UNIT], slope[s], TN
-            ).astype(BF16)
+            wd[s, at, :] = dot(mid_low[:, at], slope[s], TN).astype(BF16)
 
         times(4, one)
-
-    up_grads(0)
-    units[2].start()
-    up_grads(1)
-    units[2].after_core()
-    units[3].start()
+        start(UP, row, rows)
+
+    up_grads(0, 384)
+    flow.after(2.1)
+    up_grads(384, 384)
+    flow.after(2.1)
     acc[...] = dot(slope[0], wu[0], NT)
     times(3, lambda r: acc.__setitem__(..., acc[...] + dot(slope[r + 1], wu[r + 1], NT)))
-    units[3].after_core()
+    flow.after(2.9)
 
     def first_norm_back(i):
         at = rows_of(i, RT)
@@ -601,7 +703,7 @@
         sums[5] += fold(low.astype(F32))
 
     times(ROWS // RT, first_norm_back)
-    units[0].after_across()
+    flow.after(2.0)
 
     def out_grads(r):
         s = shard(r)
@@ -609,6 +711,7 @@
         dctx[s] = dot(wa[s, 3 * PART_D :, :], dlow[...], NT).astype(BF16)
 
     times(4, out_grads)
+    flow.after(2.7)
 
     def attend_back(r):
         s = shard(r)
@@ -629,26 +732,22 @@
 
         times(6, step)
 
-    times(2, attend_back)
-    units[0].after_pair()
-    units[1].after_across()
-    times(2, lambda r: attend_back(r + 2))
-    units[0].after_line()
-    units[1].after_pair()
-
-    def in_grads(start, rows):
+    for r in range(4):
+        attend_back(r)
+        flow.after(3.0)
+
+    def in_grads(row, rows):
         def one(r):
             s = shard(r)
-            wu[s, start : start + rows, :] = dot(qkv[s, start : start + rows, :], x[...], NN).astype(BF16)
+            wu[s, row : row + rows, :] = dot(qkv[s, row : row + rows, :], x[...], NN).astype(BF16)
 
         times(4, one)
 
-    in_grads(0, UNIT)
-    units[4].start()
-    in_grads(UNIT, PART_D)
-    units[4].after_core()
-    units[5].start()
-    small = SmallSum(peers, small_totals, small_boxes, small_line, small_sems)
+    in_grads(0, 2 * PART_D)
+    start(ATTN, 0, 2 * PART_D)
+    flow.after(2.3)
+    in_grads(2 * PART_D, PART_D)
+    flow.after(1.2)
     ones = jnp.ones((16, ROWS), BF16)
 
     def pack(r):
@@ -662,47 +761,20 @@
     for i in range(6):
         small_totals[0, 8 + i : 9 + i, :] = jnp.sum(sums[i], axis=0, keepdims=True)
     small_totals[0, 14:16, :] = jnp.zeros((2, D), F32)
+    start(ATTN, 2 * PART_D, 2 * PART_D)
     small.send(0)
-    units[5].after_core()
-    small.add(0)
-    small.send(1)
+    flow.after(1.0)
 
     def token_grads(r):
         s = shard(r)
         dz[...] += dot(qkv[s], wa[s, 0 : 3 * PART_D, :], TN)
 
-    stages = ("after_across", "after_pair", "after_line", "after_back_line", "finish")
-    done = [3, 2, 0, 0, 0, 0]
-    times(4, token_grads)
+    for r in range(2):
+        times(2, lambda i: token_grads(2 * r + i))
+        flow.after(2.9)
     gtok_copy = pltpu.make_async_copy(dz, gtok_hbm, local.at[7])
     gtok_copy.start()
-    finals, outs = (fd, fu, fa), (gd_hbm, gu_hbm, ga_hbm)
-
-    def run(n, stage):
-        assert done[n] == stage, (n, stage, done)
-        done[n] = stage + 1
-        getattr(units[n], stages[stage])()
-        if n == UNITS - 1:
-            if stage == 0:
-                small.add(1)
-                small.send(2)
-            elif stage == 1:
-                small.add(2)
-                small.send_line()
-            elif stage == 2:
-                small.add_line()
-        if stage == 4 and n % 2 == 1:
-            pltpu.make_async_copy(finals[n // 2], outs[n // 2], local.at[8 + n // 2]).start()
-
-    run(2, 0)
-    for tick in range(3, UNITS + 4):
-        for stage in reversed(range(5)):
-            n = tick - stage
-            if 0 <= n < UNITS and done[n] == stage:
-                run(n, stage)
-    for n in range(UNITS):
-        while done[n] < 5:
-            run(n, done[n])
+    flow.rest()
     small_copy = pltpu.make_async_copy(small.result(), small_hbm, local.at[11])
     small_copy.start()
     for unit in units:
@@ -742,15 +814,15 @@
         acc=wide, dz=wide, tmp=wide, dlow=low, out=low,
         sums=pltpu.VMEM((6, 8, D), F32), ub_sums=pltpu.VMEM((4, 8, D), F32), pd=whole,
         fa=final, fu=final, fd=final,
-        from_core=pltpu.VMEM((UNITS, 2, UNIT, D), BF16),
-        from_across=pltpu.VMEM((UNITS, UNIT, D), BF16),
-        from_pair=pltpu.VMEM((UNITS, PART, D), BF16),
-        from_line=pltpu.VMEM((UNITS, 3, PIECE, D), BF16),
-        from_extra=pltpu.VMEM((UNITS, max(extras, 1), PIECE, D), BF16),
+        from_core=pltpu.VMEM((2, 3 * D, D), BF16),
+        from_across=pltpu.VMEM((3 * D, D), BF16),
+        from_pair=pltpu.VMEM((3 * D // 2, D), BF16),
+        from_line=pltpu.VMEM((3, 3 * D // 8, D), BF16),
+        from_extra=pltpu.VMEM((max(extras, 1), 3 * D // 8, D), BF16),
         small_totals=pltpu.VMEM((5 + extras, SMALL, D), F32),
         small_boxes=pltpu.VMEM((3 + extras, SMALL, D), F32),
         small_line=pltpu.VMEM((4, SMALL, D), F32),
-        sems=pltpu.SemaphoreType.DMA((UNITS, 2, REDUCE_SEMS + extras)),
+        sems=pltpu.SemaphoreType.DMA((len(UNITS), 2, REDUCE_SEMS + extras)),
         small_sems=pltpu.SemaphoreType.DMA((2, SMALL_SEMS + extras)),
         sa=pltpu.SemaphoreType.DMA((2, GATHER_SEMS)),
         su=pltpu.SemaphoreType.DMA((2, GATHER_SEMS)),

time: 219 us -> 201 us (0.918)
  Pallas kernels: 194 us -> 176 us
    pallas_call x1, Pallas kernels: 194 us -> 176 us  [layer(): pl.pallas_call(functools.partial(layer_kernel, dp_size), out_shape=(jax.S...]
where the time goes in v2:
time: 201 us; the launch traced here: 200 us
  Pallas kernels  176 us (88%)
  local copies, waits for them, and re-layouts  17.1 us (9%)
  other arithmetic  6.67 us (3%)
    pallas_call x1, Pallas kernels, layer(): pl.pallas_call(functools.partial(layer_kernel, dp_size), out_shape=(jax.S...  176 us
    unnamed x39, local copies, waits for them, and re-layouts  4.22 us

profile of v2, /device:TPU:0, one launch (start us, length us, event | category | flops | bytes accessed | tf_op | source)
XLA Modules:
  0.0 200.4 jit_solution(1182147631599737354)
XLA Ops:
  0.7 0.9 select_reduce_fusion
  1.6 0.7 broadcast_compare_fusion
  2.3 0.9 copy.43
  3.2 1.2 reshape.68
  4.4 0.9 pad.12
  5.6 0.9 pad.13
  6.6 0.2 copy-done.8
  6.7 1.1 pad_maximum_fusion.a_in
  8.0 0.6 stack.31.params
  8.8 0.7 maximum_maximum_fusion.bias_in
  9.5 175.7 %shard_map.323 = (bf16[512,768]{1,0:T(8,128)(2,1)}, f32[512,768]{1,0:T(8,128)}, bf16[768,768]{1,0:T(8,128)(2,1)}, bf16[768,768]{1,0:T(8,128)(2,1)}, bf16[768,768]{1,0:T(8,128)(2,1)}, /*index=5*/f32[16,768]{1,0:T(8,128)}) custom-call(bf16[512,768]{1,0:T(8,128)(2,1)} %bitcast.22, bf16[512,768]{1,0:T(8,128)(2,1)} %bitcast.23, f32[512,1]{1,0:T(8,128)} %bitcast.25, ...), custom_call_target="tpu_custom_call" | custom-call | tf_op jit(solution)/shard_map/pallas_call | solution.py:833
  185.2 1.8 slice_reduce_fusion
  186.9 1.4 fusion.2
  188.3 1.4 convert_element_type.13
  189.7 1.2 slice_bitcast_fusion
  191.0 0.6 copy-done
  191.6 0.9 slice.69
  192.5 0.2 convert_bitcast_fusion
  192.7 2.0 copy.41
  194.6 1.4 slice.65
  196.1 1.2 reshape.77
  197.3 0.5 copy-done.1
  197.8 1.6 convert_element_type.14
  199.4 1.0 reshape.75
  (52 shorter events, 0.6 us)
Async XLA Ops:
  2.3 3.1 %copy-start.3 = (bf16[456,768]{1,0:T(8,128)(2,1)S(1)}, bf16[456,768]{1,0:T(8,128)(2,1)}, u32[]{:S(2)}) copy-start(bf16[456,768]{1,0:T(8,128)(2,1)} %param.39) | copy-start | bytes 2101252
  5.4 1.2 copy-start.5
  5.4 1.2 copy-start.6
  5.4 1.2 copy-start.7
  5.4 1.4 copy-start.8
  5.5 2.3 %copy-start.9 = (f32[768]{0:T(1024)S(1)}, f32[768]{0:T(1024)}, u32[]{:S(2)}) copy-start(f32[768]{0:T(1024)} %param.30) | copy-start | bytes 9220
  5.5 2.3 %copy-start.10 = (f32[768]{0:T(1024)S(1)}, f32[768]{0:T(1024)}, u32[]{:S(2)}) copy-start(f32[768]{0:T(1024)} %param.31) | copy-start | bytes 9220
  5.6 2.3 %copy-start.11 = (f32[768]{0:T(1024)S(1)}, f32[768]{0:T(1024)}, u32[]{:S(2)}) copy-start(f32[768]{0:T(1024)} %param.32) | copy-start | bytes 9220
  5.6 2.3 %copy-start.12 = (f32[768]{0:T(1024)S(1)}, f32[768]{0:T(1024)}, u32[]{:S(2)}) copy-start(f32[768]{0:T(1024)} %param.36) | copy-start | bytes 9220
  5.6 2.3 %copy-start.13 = (f32[768]{0:T(1024)S(1)}, f32[768]{0:T(1024)}, u32[]{:S(2)}) copy-start(f32[768]{0:T(1024)} %param.37) | copy-start | bytes 9220
  6.5 1.4 copy-start.14
  6.5 2.1 %copy-start.16 = (f32[192]{0:T(256)S(1)}, f32[192]{0:T(256)}, u32[]{:S(2)}) copy-start(f32[192]{0:T(256)} %param.28) | copy-start | bytes 2308
  6.5 2.1 %copy-start.17 = (f32[192]{0:T(256)S(1)}, f32[192]{0:T(256)}, u32[]{:S(2)}) copy-start(f32[192]{0:T(256)} %param.25) | copy-start | bytes 2308
  6.5 2.2 %copy-start.15 = (f32[768]{0:T(1024)S(1)}, f32[768]{0:T(1024)}, u32[]{:S(2)}) copy-start(f32[768]{0:T(1024)} %param.34) | copy-start | bytes 9220
  189.7 1.9 copy-start
  189.7 2.8 %copy-start.2 = (bf16[768,768]{1,0:T(8,128)(2,1)S(1)}, bf16[768,768]{1,0:T(8,128)(2,1)}, u32[]{:S(2)}) copy-start(bf16[768,768]{1,0:T(8,128)(2,1)} %get-tuple-element.28) | copy-start | bytes 3538948
  196.1 1.7 copy-start.1
  197.8 1.6 copy-start.4
